TPU v7x, 128 devices: a whole 4x4x4 slice. The times are simulated.
128 devices in a mesh: row: 16 (over x, y_hi, core), col: 8 (over z, y_lo).
Axes of the slice: x: 4, y: 4 (y_hi: 2, y_lo: 2; y = y_hi * 2 + y_lo), z: 4, core: 2. Of those that a mesh axis runs over, the one named last changes fastest.
Arguments:
- counts: int32 [16384, 16384], P('row', 'col'), may hold values from 0 to 33, as said below
- row_emb: float32 [256, 16384], P('col', 'row'), may hold values from -2 to 2
- col_emb: float32 [256, 16384], P('row', 'col'), may hold values from -2 to 2
- row_accum: float32 [256, 16384], P('col', 'row'), may hold values from 100 to 10000
- col_accum: float32 [256, 16384], P('row', 'col'), may hold values from 100 to 10000
Outputs:
- new_row_emb: float32 [256, 16384], P('col', 'row')
- new_col_emb: float32 [256, 16384], P('row', 'col')
Inputs may be any that keep to these rules, and one draw needn't show every extreme that they name: `counts`: every row word and every column word has a positive count with some partner.
All inputs are finite; a program needn't handle non-finite values.
Results may differ from a plain program's by a relative error of at most 0.0015.
Values may be sent and summed in bfloat16 or wider, within the bound.
No kernel may reach another device: no remote copies, remote signals or barrier semaphores. Data moves between devices by JAX's collectives and lax.ppermute only.
A program may use at most 64 MiB of HBM per device.

v0:
```python
import jax
import jax.numpy as jnp
from jax import lax
from jax.sharding import PartitionSpec as P

SWEEPS = 2


def copy_for_each(value, axis):
    length = lax.axis_size(axis)
    return lax.all_to_all(
        jnp.broadcast_to(value[None], (length, *value.shape)), axis, 0, 0, tiled=True
    )


def in_order(tiles, dim):
    tiles = jnp.moveaxis(tiles, 0, dim)
    lengths = tiles.shape
    return tiles.reshape(*lengths[:dim], lengths[dim] * lengths[dim + 1], *lengths[dim + 2 :])


def gathered_copies(value, axis, dim):
    tiles = copy_for_each(value, axis)
    return in_order(tiles, dim)


def split_up(value, dim, length):
    before, after = (value.shape[:dim], value.shape[dim + 1 :])
    return jnp.moveaxis(value.reshape(*before, length, -1, *after), dim, 0)


def sent_and_summed(value, axis, dim):
    tiles = split_up(value, dim, lax.axis_size(axis))
    arrived = lax.all_to_all(tiles, axis, split_axis=0, concat_axis=0, tiled=True)
    return arrived.astype(jnp.float32).sum(axis=0)


def over_copies(value, axis):
    everything = copy_for_each(value, axis)
    return jnp.sum(everything, axis=0)


def sweep_once(row_emb, col_emb, row_accum, col_accum, positive, target, weight):
    row_half = row_emb.astype(jnp.bfloat16)
    col_half = col_emb.astype(jnp.bfloat16)
    row_block = gathered_copies(row_half, "col", 0)
    col_block = lax.all_gather(col_half, "row", axis=0, tiled=True)
    scores = lax.dot_general(
        row_block, col_block, (((0,), (0,)), ((), ())), preferred_element_type=jnp.float32
    )
    errors = scores - target
    grads = jnp.where(positive, weight * errors, jax.nn.sigmoid(errors)).astype(jnp.bfloat16)
    piece = col_block
    row_grad = sent_and_summed(
        lax.dot_general(
            piece, grads, (((1,), (1,)), ((), ())), preferred_element_type=jnp.float32
        ).astype(jnp.bfloat16),
        "col",
        0,
    )
    piece = row_block
    col_grad = sent_and_summed(
        jnp.dot(piece, grads, preferred_element_type=jnp.float32).astype(jnp.bfloat16), "row", 0
    )
    row_accum = row_accum + row_grad * row_grad
    row_emb = row_emb - 0.05 * row_grad / jnp.sqrt(row_accum)
    col_accum = col_accum + col_grad * col_grad
    col_emb = col_emb - 0.05 * col_grad / jnp.sqrt(col_accum)
    return (row_emb, col_emb, row_accum, col_accum)


def on_device(counts, row_emb, col_emb, row_accum, col_accum):
    values = counts.astype(jnp.float32)
    local_rows = jnp.sum(values, axis=1)
    local_cols = jnp.sum(values, axis=0)
    row_marg = over_copies(local_rows, "col")
    col_marg = over_copies(local_cols, "row")
    total = over_copies(jnp.sum(row_marg), "row")
    target = (
        jnp.log(jnp.maximum(values, 1.0))
        + jnp.log(total)
        - jnp.log(row_marg)[:, None]
        - jnp.log(col_marg)[None, :]
    )
    weight = 0.1 + 0.25 * jnp.sqrt(values)
    positive = counts > 0
    for sweep in range(SWEEPS):
        row_emb, col_emb, row_accum, col_accum = sweep_once(
            row_emb, col_emb, row_accum, col_accum, positive, target, weight
        )
    return (row_emb, col_emb)


def solution(mesh):
    in_specs = (P("row", "col"), P("col", "row"), P("row", "col"), P("col", "row"), P("row", "col"))
    out_specs = (P("col", "row"), P("row", "col"))
    return jax.shard_map(
        on_device, mesh=mesh, in_specs=in_specs, out_specs=out_specs, check_vma=False
    )
```

profile of v0, /device:TPU:1, one launch (start us, length us, event | category | flops | bytes accessed | tf_op | source)
XLA Modules:
  0.0 206.4 jit_solution(5882931983976948135)
XLA Ops:
  7.2 0.0 copy-start
  7.2 0.0 all-gather.3.cloned.1.call-start
  7.2 1.6 convert_element_type.53
  8.8 0.0 all-gather.3.cloned.1.call-update
  8.8 4.6 %convert_reduce_fusion.1 = (f32[1024]{0:T(1024)S(1)}, f32[2048]{0:T(1024)S(1)}) fusion(s32[1024,2048]{1,0:T(8,128)} %param.5), kind=kLoop, calls=%fused_computation.5 | loop fusion | flops 6288384 | bytes 8400896 | tf_op jit(solution)/shard_map/reduce_sum | solution.py:74
  13.5 11.8 %all_to_all.48 = f32[8,1,1024]{2,1,0:T(1,128)S(1)} all-to-all(f32[8,1,1024]{2,1,0:T(1,128)S(1)} %broadcast_in_dim.11), channel_id=1, replica_groups=mesh['row'=16,'col'=8] {'col'}, dimensions={0} | all-to-all | bytes 65536 | tf_op jit(solution)/shard_map/all_to_all | solution.py:11
  25.3 0.7 fusion.2
  25.9 0.6 broadcast_in_dim.12
  26.6 15.6 %all_to_all.49 = f32[16,1,1]{2,1,0:T(1,128)S(1)} all-to-all(f32[16,1,1]{2,1,0:T(1,128)S(1)} %broadcast_in_dim.12), channel_id=1, replica_groups=mesh['row'=16,'col'=8] {'row'}, dimensions={0} | all-to-all | bytes 128 | tf_op jit(solution)/shard_map/all_to_all | solution.py:11
  42.1 0.7 broadcast_in_dim.13
  42.9 4.0 %all-to-all-start.3 = ((f32[16,1,2048]{2,1,0:T(1,128)}), f32[16,1,2048]{2,1,0:T(1,128)S(1)}, u32[]{:S(2)}, u32[]{:S(2)}) async-start(f32[16,1,2048]{2,1,0:T(1,128)} %broadcast_in_dim.13), calls=%async_computation.3 | async-start | bytes 262144 | tf_op jit(solution)/shard_map/all_to_all | solution.py:11
  46.8 0.0 copy-done
  46.9 8.2 %all-to-all-done.3 = f32[16,1,2048]{2,1,0:T(1,128)S(1)} async-done(((f32[16,1,2048]{2,1,0:T(1,128)}), f32[16,1,2048]{2,1,0:T(1,128)S(1)}, u32[]{:S(2)}, u32[]{:S(2)}) %all-to-all-start.3) | async-done | bytes 131104 | tf_op jit(solution)/shard_map/all_to_all | solution.py:11
  55.1 0.8 broadcast_in_dim.10
  55.9 3.5 %all-to-all-start = ((bf16[8,32,1024]{2,1,0:T(8,128)(2,1)}), bf16[8,32,1024]{2,1,0:T(8,128)(2,1)S(1)}, u32[]{:S(2)}, u32[]{:S(2)}) async-start(bf16[8,32,1024]{2,1,0:T(8,128)(2,1)} %broadcast_in_dim.10), calls=%async_computation | async-start | bytes 1048576 | tf_op jit(solution)/shard_map/all_to_all | solution.py:11
  59.4 0.0 all-gather.5.cloned.1.call-start
  59.5 0.6 reduce_sum.92
  60.8 0.1 reduce_sum.95
  60.9 8.0 %all-to-all-done = bf16[8,32,1024]{2,1,0:T(8,128)(2,1)S(1)} async-done(((bf16[8,32,1024]{2,1,0:T(8,128)(2,1)}), bf16[8,32,1024]{2,1,0:T(8,128)(2,1)S(1)}, u32[]{:S(2)}, u32[]{:S(2)}) %all-to-all-start) | async-done | bytes 524320 | tf_op jit(solution)/shard_map/all_to_all | solution.py:11
  68.9 0.0 all-gather.3.cloned.1.call-done
  68.9 12.8 %select_convert_fusion.1 = bf16[1024,2048]{1,0:T(8,128)(2,1)S(1)} fusion(s32[1024,2048]{1,0:T(8,128)} %param.5, bf16[256,1024]{1,0:T(8,128)(2,1)S(1)} %bitcast.23, bf16[256,2048]{1,0:T(8,128)(2,1)} %all-gather.3.cloned.1.call-done, f32[2048]{0:T(1024)S(1)} %log.23, f32[1024]{0:T(1024)S(1)} %log.22, f32[]{:T(128)S(6)} %log.21), kind=kOutput, calls=%fused_computation.1 | convolution fusion | flops 1105199104 | bytes 14168068 | tf_op jit(solution)/shard_map/dot_general | solution.py:48
  81.8 0.0 copy-start.6
  81.8 0.0 copy-start.1
  81.8 0.0 copy-start.3
  81.8 0.0 copy-start.4
  81.8 0.0 copy-start.2
  81.8 1.3 convolution_convert_fusion
  83.1 21.2 %all_to_all.50 = bf16[16,16,2048]{2,1,0:T(8,128)(2,1)S(1)} all-to-all(bf16[16,16,2048]{2,1,0:T(8,128)(2,1)S(1)} %bitcast.22), channel_id=1, replica_groups=mesh['row'=16,'col'=8] {'row'}, dimensions={0} | all-to-all | bytes 2097152 | tf_op jit(solution)/shard_map/all_to_all | solution.py:34
  104.3 0.1 convert_reduce_fusion.3
  104.4 0.0 copy-done.6
  104.4 0.0 copy-done.1
  104.4 0.0 copy-done.3
  104.4 0.7 fusion.1
  105.1 0.0 all-gather.5.cloned.1.call-update
  105.1 0.0 copy-done.4
  105.1 3.5 %convolution_convert_fusion.3 = bf16[1024,256]{0,1:T(8,128)(2,1)S(1)} fusion(bf16[1024,2048]{1,0:T(8,128)(2,1)} %copy-done.6, bf16[256,2048]{1,0:T(8,128)(2,1)S(1)} %copy-done.4), kind=kOutput, calls=%fused_computation.12 | convolution fusion | flops 1074003968 | bytes 5767168 | tf_op jit(solution)/shard_map/dot_general | solution.py:55
  108.6 12.2 %all_to_all.51 = bf16[8,32,1024]{2,1,0:T(8,128)(2,1)S(1)} all-to-all(bf16[8,32,1024]{2,1,0:T(8,128)(2,1)S(1)} %bitcast.27), channel_id=1, replica_groups=mesh['row'=16,'col'=8] {'col'}, dimensions={0} | all-to-all | bytes 1048576 | tf_op jit(solution)/shard_map/all_to_all | solution.py:34
  120.8 0.1 convert_reduce_fusion.5
  120.9 0.0 copy-done.2
  120.9 0.1 broadcast_in_dim.14
  121.0 10.8 %all_to_all.52 = bf16[8,32,1024]{2,1,0:T(8,128)(2,1)S(1)} all-to-all(bf16[8,32,1024]{2,1,0:T(8,128)(2,1)S(1)} %broadcast_in_dim.14), channel_id=1, replica_groups=mesh['row'=16,'col'=8] {'col'}, dimensions={0} | all-to-all | bytes 1048576 | tf_op jit(solution)/shard_map/all_to_all | solution.py:11
  131.8 14.3 %all-gather.5.cloned.1.call-done = bf16[256,2048]{1,0:T(8,128)(2,1)} async-done(((bf16[16,2048]{1,0:T(8,128)(2,1)}), bf16[256,2048]{1,0:T(8,128)(2,1)}) %all-gather.5.cloned.1.call-update) | async-done | bytes 1048592 | tf_op jit(solution)/shard_map/all_gather | solution.py:47
  146.1 0.0 copy-start.5
  146.1 13.2 %select_convert_fusion = bf16[1024,2048]{1,0:T(8,128)(2,1)S(1)} fusion(s32[1024,2048]{1,0:T(8,128)} %param.5, bf16[256,1024]{1,0:T(8,128)(2,1)S(1)} %bitcast.25, bf16[256,2048]{1,0:T(8,128)(2,1)} %all-gather.5.cloned.1.call-done, f32[2048]{0:T(1024)S(1)} %log.23, f32[1024]{0:T(1024)S(1)} %log.22, f32[]{:T(128)S(6)} %log.21), kind=kOutput, calls=%fused_computation | convolution fusion | flops 1105199104 | bytes 14168068 | tf_op jit(solution)/shard_map/dot_general | solution.py:48
  159.3 0.0 copy-done.5
  159.4 0.0 copy-start.7
  159.4 2.1 %convolution_convert_fusion.2 = bf16[256,1024]{1,0:T(8,128)(2,1)} fusion(bf16[256,2048]{1,0:T(8,128)(2,1)S(1)} %copy-done.5, bf16[1024,2048]{1,0:T(8,128)(2,1)S(1)} %select_convert_fusion), kind=kOutput, calls=%fused_computation.11 | convolution fusion | flops 1074003968 | bytes 5767168 | tf_op jit(solution)/shard_map/dot_general | solution.py:55
  161.5 0.0 copy-done.7
  161.5 4.2 %all-to-all-start.7 = ((bf16[8,32,1024]{2,1,0:T(8,128)(2,1)}), bf16[8,32,1024]{2,1,0:T(8,128)(2,1)S(1)}, u32[]{:S(2)}, u32[]{:S(2)}) async-start(bf16[8,32,1024]{2,1,0:T(8,128)(2,1)} %bitcast.6), calls=%async_computation.7 | async-start | bytes 1048576 | tf_op jit(solution)/shard_map/all_to_all | solution.py:34
  165.6 4.4 %convolution_convert_fusion.1 = bf16[256,2048]{1,0:T(8,128)(2,1)} fusion(bf16[256,1024]{1,0:T(8,128)(2,1)S(1)} %bitcast.26, bf16[1024,2048]{1,0:T(8,128)(2,1)} %copy-done.7), kind=kOutput, calls=%fused_computation.8 | convolution fusion | flops 1074266112 | bytes 5767168 | tf_op jit(solution)/shard_map/dot_general | solution.py:63
  170.1 4.9 %all-to-all-done.7 = bf16[8,32,1024]{2,1,0:T(8,128)(2,1)S(1)} async-done(((bf16[8,32,1024]{2,1,0:T(8,128)(2,1)}), bf16[8,32,1024]{2,1,0:T(8,128)(2,1)S(1)}, u32[]{:S(2)}, u32[]{:S(2)}) %all-to-all-start.7) | async-done | bytes 524320 | tf_op jit(solution)/shard_map/all_to_all | solution.py:34
  175.0 6.8 %all-to-all-start.8 = ((bf16[16,16,2048]{2,1,0:T(8,128)(2,1)}), bf16[16,16,2048]{2,1,0:T(8,128)(2,1)S(1)}, u32[]{:S(2)}, u32[]{:S(2)}) async-start(bf16[16,16,2048]{2,1,0:T(8,128)(2,1)} %bitcast.7), calls=%async_computation.8 | async-start | bytes 2097152 | tf_op jit(solution)/shard_map/all_to_all | solution.py:34
  181.8 0.1 convert_reduce_fusion.4
  181.9 0.7 multiply_subtract_fusion.1
  182.6 16.1 %all-to-all-done.8 = bf16[16,16,2048]{2,1,0:T(8,128)(2,1)S(1)} async-done(((bf16[16,16,2048]{2,1,0:T(8,128)(2,1)}), bf16[16,16,2048]{2,1,0:T(8,128)(2,1)S(1)}, u32[]{:S(2)}, u32[]{:S(2)}) %all-to-all-start.8) | async-done | bytes 1048608 | tf_op jit(solution)/shard_map/all_to_all | solution.py:34
  198.7 0.1 convert_reduce_fusion.2
  198.9 0.7 multiply_subtract_fusion
  (5 shorter events, 0.1 us)
Async XLA Ops:
  7.2 39.7 %copy-start = (f32[32,1024]{1,0:T(8,128)S(1)}, f32[32,1024]{1,0:T(8,128)}, u32[]{:S(2)}) copy-start(f32[32,1024]{1,0:T(8,128)} %param.6) | copy-start | bytes 393220
  7.2 61.8 %all-gather.3.cloned.1.call-start = ((), (), s32[]{:S(2)}) async-start(), calls=%async_computation.9 | async-start | bytes 1114112 | tf_op jit(solution)/shard_map/all_gather | solution.py:47
  42.9 12.2 %all-to-all-start.3 = ((f32[16,1,2048]{2,1,0:T(1,128)}), f32[16,1,2048]{2,1,0:T(1,128)S(1)}, u32[]{:S(2)}, u32[]{:S(2)}) async-start(f32[16,1,2048]{2,1,0:T(1,128)} %broadcast_in_dim.13), calls=%async_computation.3 | async-start | bytes 262144 | tf_op jit(solution)/shard_map/all_to_all | solution.py:11
  55.9 13.0 %all-to-all-start = ((bf16[8,32,1024]{2,1,0:T(8,128)(2,1)}), bf16[8,32,1024]{2,1,0:T(8,128)(2,1)S(1)}, u32[]{:S(2)}, u32[]{:S(2)}) async-start(bf16[8,32,1024]{2,1,0:T(8,128)(2,1)} %broadcast_in_dim.10), calls=%async_computation | async-start | bytes 1048576 | tf_op jit(solution)/shard_map/all_to_all | solution.py:11
  59.4 86.7 %all-gather.5.cloned.1.call-start = ((), (), s32[]{:S(2)}) async-start(), calls=%async_computation.10 | async-start | bytes 1114112 | tf_op jit(solution)/shard_map/all_gather | solution.py:47
  81.8 22.6 %copy-start.6 = (bf16[1024,2048]{1,0:T(8,128)(2,1)}, bf16[1024,2048]{1,0:T(8,128)(2,1)S(1)}, u32[]{:S(2)}) copy-start(bf16[1024,2048]{1,0:T(8,128)(2,1)S(1)} %select_convert_fusion.1) | copy-start | bytes 12582916
  81.8 22.6 %copy-start.1 = (f32[16,2048]{1,0:T(8,128)S(1)}, f32[16,2048]{1,0:T(8,128)}, u32[]{:S(2)}) copy-start(f32[16,2048]{1,0:T(8,128)} %param.7) | copy-start | bytes 393220
  81.8 22.6 %copy-start.3 = (f32[16,2048]{1,0:T(8,128)S(1)}, f32[16,2048]{1,0:T(8,128)}, u32[]{:S(2)}) copy-start(f32[16,2048]{1,0:T(8,128)} %param.9) | copy-start | bytes 393220
  81.8 23.3 %copy-start.4 = (bf16[256,2048]{1,0:T(8,128)(2,1)S(1)}, bf16[256,2048]{1,0:T(8,128)(2,1)}, u32[]{:S(2)}) copy-start(bf16[256,2048]{1,0:T(8,128)(2,1)} %all-gather.3.cloned.1.call-done) | copy-start | bytes 3145732
  81.8 39.1 %copy-start.2 = (f32[32,1024]{1,0:T(8,128)S(1)}, f32[32,1024]{1,0:T(8,128)}, u32[]{:S(2)}) copy-start(f32[32,1024]{1,0:T(8,128)} %param.8) | copy-start | bytes 393220
  146.1 13.2 %copy-start.5 = (bf16[256,2048]{1,0:T(8,128)(2,1)S(1)}, bf16[256,2048]{1,0:T(8,128)(2,1)}, u32[]{:S(2)}) copy-start(bf16[256,2048]{1,0:T(8,128)(2,1)} %all-gather.5.cloned.1.call-done) | copy-start | bytes 3145732
  159.4 2.1 %copy-start.7 = (bf16[1024,2048]{1,0:T(8,128)(2,1)}, bf16[1024,2048]{1,0:T(8,128)(2,1)S(1)}, u32[]{:S(2)}) copy-start(bf16[1024,2048]{1,0:T(8,128)(2,1)S(1)} %select_convert_fusion) | copy-start | bytes 12582916
  161.5 13.5 %all-to-all-start.7 = ((bf16[8,32,1024]{2,1,0:T(8,128)(2,1)}), bf16[8,32,1024]{2,1,0:T(8,128)(2,1)S(1)}, u32[]{:S(2)}, u32[]{:S(2)}) async-start(bf16[8,32,1024]{2,1,0:T(8,128)(2,1)} %bitcast.6), calls=%async_computation.7 | async-start | bytes 1048576 | tf_op jit(solution)/shard_map/all_to_all | solution.py:34
  175.0 23.8 %all-to-all-start.8 = ((bf16[16,16,2048]{2,1,0:T(8,128)(2,1)}), bf16[16,16,2048]{2,1,0:T(8,128)(2,1)S(1)}, u32[]{:S(2)}, u32[]{:S(2)}) async-start(bf16[16,16,2048]{2,1,0:T(8,128)(2,1)} %bitcast.7), calls=%async_computation.8 | async-start | bytes 2097152 | tf_op jit(solution)/shard_map/all_to_all | solution.py:34
Sparse Core Ops, SparseCore 0:
  10.9 48.3 all-gather.2
  105.2 40.8 all-gather.4
where the time goes:
time: 207 us; the launch traced here: 206 us
  blocking collectives  71.5 us (35%)
  waiting for transfers between devices  51.6 us (25%)
  matrix products  37.3 us (18%)
  starting transfers between devices  18.5 us (9%)
  between operations  15 us (7%)
  other arithmetic  10.2 us (5%)
  local copies, waits for them, and re-layouts  2.34 us (1%)
    all_to_all x3, blocking collectives, copy_for_each(): lax.all_to_all(jnp.broadcast_to(value[None], (length, *value.shape)), axi...  38.1 us
    all_to_all x2, blocking collectives, sent_and_summed(): lax.all_to_all(tiles, axis, split_axis=0, concat_axis=0, tiled=True)  33.3 us
    dot_general x2, matrix products, sweep_once(): lax.dot_general(row_block, col_block, (((0,), (0,)), ((), ())), preferred...  26.1 us
    all_to_all x2, waiting for transfers between devices, sent_and_summed(): lax.all_to_all(tiles, axis, split_axis=0, concat_axis=0, tiled=True)  21 us
    all_to_all x2, waiting for transfers between devices, copy_for_each(): lax.all_to_all(jnp.broadcast_to(value[None], (length, *value.shape)), axi...  16.2 us
    all_gather x2, waiting for transfers between devices, sweep_once(): col_block = lax.all_gather(col_half, 'row', axis=0, tiled=True)  14.3 us
    all_to_all x2, starting transfers between devices, sent_and_summed(): lax.all_to_all(tiles, axis, split_axis=0, concat_axis=0, tiled=True)  11 us
    all_to_all x2, starting transfers between devices, copy_for_each(): lax.all_to_all(jnp.broadcast_to(value[None], (length, *value.shape)), axi...  7.46 us
  transfers between devices with their start and end apart: 6, of which 5 were waited for; matrix products, arithmetic and copies ran while one was open for 8% of the time, Pallas kernels for 0%

commit v1 on v0

--- a/solution.py
+++ b/solution.py
@@ -44,7 +44,9 @@
     row_half = row_emb.astype(jnp.bfloat16)
     col_half = col_emb.astype(jnp.bfloat16)
     row_block = gathered_copies(row_half, "col", 0)
-    col_block = lax.all_gather(col_half, "row", axis=0, tiled=True)
+    col_block = jnp.concatenate(
+        lax.all_to_all(jnp.stack([col_half] * lax.axis_size("row")), "row", 0, 0), axis=0
+    )
     scores = lax.dot_general(
         row_block, col_block, (((0,), (0,)), ((), ())), preferred_element_type=jnp.float32
     )

time: 207 us -> 222 us (1.072)
  waiting for transfers between devices: 51.6 us -> 83.6 us
  blocking collectives: 71.5 us -> 50 us
  starting transfers between devices: 18.5 us -> 34.4 us
  between operations: 15 us -> 1.53 us
    all_to_all x2 -> x4, waiting for transfers between devices: 21 us -> 42.2 us  [sent_and_summed(): lax.all_to_all(tiles, axis, split_axis=0, concat_axis=0, tiled=True)]
    all_to_all x0 -> x1, waiting for transfers between devices: none -> 15.6 us  [sweep_once(): lax.all_to_all(jnp.stack([col_half] * lax.axis_size('row')), 'row', 0, 0)]
    all_gather x2 -> x0, waiting for transfers between devices: 14.3 us -> none  [sweep_once(): col_block = lax.all_gather(col_half, 'row', axis=0, tiled=True)]
    all_to_all x3 -> x2, blocking collectives: 38.1 us -> 27.3 us  [copy_for_each(): lax.all_to_all(jnp.broadcast_to(value[None], (length, *value.shape)), axi...]
    all_to_all x2 -> x1, blocking collectives: 33.3 us -> 22.6 us  [sweep_once(): lax.all_to_all(jnp.stack([col_half] * lax.axis_size('row')), 'row', 0, 0)]
    all_to_all x2 -> x3, waiting for transfers between devices: 16.2 us -> 25.8 us  [copy_for_each(): lax.all_to_all(jnp.broadcast_to(value[None], (length, *value.shape)), axi...]
    all_to_all x2 -> x4, starting transfers between devices: 11 us -> 18.4 us  [sent_and_summed(): lax.all_to_all(tiles, axis, split_axis=0, concat_axis=0, tiled=True)]
    all_to_all x0 -> x1, starting transfers between devices: none -> 5.06 us  [sweep_once(): lax.all_to_all(jnp.stack([col_half] * lax.axis_size('row')), 'row', 0, 0)]
  transfers between devices with their start and end apart: 6 -> 8, of which waited for: 5 -> 8; matrix products, arithmetic and copies ran while one was open for 8% -> 5% of each run, Pallas kernels for 0% -> 0%
where the time goes in v1:
time: 222 us; the launch traced here: 221 us
  waiting for transfers between devices  83.6 us (38%)
  blocking collectives  50 us (23%)
  matrix products  38.8 us (17%)
  starting transfers between devices  34.4 us (15%)
  other arithmetic  8.05 us (4%)
  local copies, waits for them, and re-layouts  4.34 us (2%)
    all_to_all x4, waiting for transfers between devices, sent_and_summed(): lax.all_to_all(tiles, axis, split_axis=0, concat_axis=0, tiled=True)  42.2 us
    all_to_all x2, blocking collectives, copy_for_each(): lax.all_to_all(jnp.broadcast_to(value[None], (length, *value.shape)), axi...  27.3 us
    all_to_all x3, waiting for transfers between devices, copy_for_each(): lax.all_to_all(jnp.broadcast_to(value[None], (length, *value.shape)), axi...  25.8 us
    dot_general x2, matrix products, sweep_once(): lax.dot_general(row_block, col_block, (((0,), (0,)), ((), ())), preferred...  25.7 us
    all_to_all x1, blocking collectives, sweep_once(): lax.all_to_all(jnp.stack([col_half] * lax.axis_size('row')), 'row', 0, 0)  22.6 us
    all_to_all x4, starting transfers between devices, sent_and_summed(): lax.all_to_all(tiles, axis, split_axis=0, concat_axis=0, tiled=True)  18.4 us
    all_to_all x1, waiting for transfers between devices, sweep_once(): lax.all_to_all(jnp.stack([col_half] * lax.axis_size('row')), 'row', 0, 0)  15.6 us
    all_to_all x3, starting transfers between devices, copy_for_each(): lax.all_to_all(jnp.broadcast_to(value[None], (length, *value.shape)), axi...  11 us
  transfers between devices with their start and end apart: 8, of which 8 were waited for; matrix products, arithmetic and copies ran while one was open for 5% of the time, Pallas kernels for 0%

profile of v1, /device:TPU:1, one launch (start us, length us, event | category | flops | bytes accessed | tf_op | source)
XLA Modules:
  0.0 220.7 jit_solution(15094790278284111871)
XLA Ops:
  0.6 0.0 copy-start
  0.6 0.0 copy-start.1
  0.6 4.7 %convert_reduce_fusion.1 = (f32[1024]{0:T(1024)S(1)}, f32[2048]{0:T(1024)S(1)}) fusion(s32[1024,2048]{1,0:T(8,128)} %param.5), kind=kLoop, calls=%fused_computation.5 | loop fusion | flops 6288384 | bytes 8400896 | tf_op jit(solution)/shard_map/reduce_sum | solution.py:76
  5.4 11.8 %all_to_all.58 = f32[8,1,1024]{2,1,0:T(1,128)S(1)} all-to-all(f32[8,1,1024]{2,1,0:T(1,128)S(1)} %broadcast_in_dim.11), channel_id=1, replica_groups=mesh['row'=16,'col'=8] {'col'}, dimensions={0} | all-to-all | bytes 65536 | tf_op jit(solution)/shard_map/all_to_all | solution.py:11
  17.1 0.7 fusion.2
  17.8 0.6 broadcast_in_dim.12
  18.5 15.6 %all_to_all.59 = f32[16,1,1]{2,1,0:T(1,128)S(1)} all-to-all(f32[16,1,1]{2,1,0:T(1,128)S(1)} %broadcast_in_dim.12), channel_id=1, replica_groups=mesh['row'=16,'col'=8] {'row'}, dimensions={0} | all-to-all | bytes 128 | tf_op jit(solution)/shard_map/all_to_all | solution.py:11
  34.0 0.7 broadcast_in_dim.13
  34.7 4.0 %all-to-all-start.4 = ((f32[16,1,2048]{2,1,0:T(1,128)}), f32[16,1,2048]{2,1,0:T(1,128)S(1)}, u32[]{:S(2)}, u32[]{:S(2)}) async-start(f32[16,1,2048]{2,1,0:T(1,128)} %broadcast_in_dim.13), calls=%async_computation.4 | async-start | bytes 262144 | tf_op jit(solution)/shard_map/all_to_all | solution.py:11
  38.7 0.0 copy-done
  38.7 7.7 %all-to-all-done.4 = f32[16,1,2048]{2,1,0:T(1,128)S(1)} async-done(((f32[16,1,2048]{2,1,0:T(1,128)}), f32[16,1,2048]{2,1,0:T(1,128)S(1)}, u32[]{:S(2)}, u32[]{:S(2)}) %all-to-all-start.4) | async-done | bytes 131104 | tf_op jit(solution)/shard_map/all_to_all | solution.py:11
  46.4 0.8 broadcast_in_dim.10
  47.3 3.5 %all-to-all-start = ((bf16[8,32,1024]{2,1,0:T(8,128)(2,1)}), bf16[8,32,1024]{2,1,0:T(8,128)(2,1)S(1)}, u32[]{:S(2)}, u32[]{:S(2)}) async-start(bf16[8,32,1024]{2,1,0:T(8,128)(2,1)} %broadcast_in_dim.10), calls=%async_computation | async-start | bytes 1048576 | tf_op jit(solution)/shard_map/all_to_all | solution.py:11
  50.8 0.0 copy-done.1
  50.8 9.3 %all-to-all-done = bf16[8,32,1024]{2,1,0:T(8,128)(2,1)S(1)} async-done(((bf16[8,32,1024]{2,1,0:T(8,128)(2,1)}), bf16[8,32,1024]{2,1,0:T(8,128)(2,1)S(1)}, u32[]{:S(2)}, u32[]{:S(2)}) %all-to-all-start) | async-done | bytes 524320 | tf_op jit(solution)/shard_map/all_to_all | solution.py:11
  60.1 1.1 stack.4
  61.2 5.1 %all-to-all-start.1 = ((bf16[16,16,2048]{2,1,0:T(8,128)(2,1)}), bf16[16,16,2048]{2,1,0:T(8,128)(2,1)S(1)}, u32[]{:S(2)}, u32[]{:S(2)}) async-start(bf16[16,16,2048]{2,1,0:T(8,128)(2,1)} %stack.4), calls=%async_computation.1 | async-start | bytes 2097152 | tf_op jit(solution)/shard_map/all_to_all | solution.py:48
  66.3 0.6 reduce_sum.92
  67.6 0.1 reduce_sum.95
  67.7 15.6 %all-to-all-done.1 = bf16[16,16,2048]{2,1,0:T(8,128)(2,1)S(1)} async-done(((bf16[16,16,2048]{2,1,0:T(8,128)(2,1)}), bf16[16,16,2048]{2,1,0:T(8,128)(2,1)S(1)}, u32[]{:S(2)}, u32[]{:S(2)}) %all-to-all-start.1) | async-done | bytes 1048608 | tf_op jit(solution)/shard_map/all_to_all | solution.py:48
  83.4 12.9 %select_convert_fusion.1 = bf16[1024,2048]{1,0:T(8,128)(2,1)S(1)} fusion(s32[1024,2048]{1,0:T(8,128)} %param.5, bf16[256,1024]{1,0:T(8,128)(2,1)S(1)} %bitcast.28, bf16[256,2048]{1,0:T(8,128)(2,1)S(1)} %bitcast.24, f32[2048]{0:T(1024)S(1)} %log.23, f32[1024]{0:T(1024)S(1)} %log.22, f32[]{:T(128)S(6)} %log.21), kind=kOutput, calls=%fused_computation.1 | convolution fusion | flops 1105199104 | bytes 14168068 | tf_op jit(solution)/shard_map/dot_general | solution.py:50
  96.2 0.0 copy-start.5
  96.3 0.0 copy-start.2
  96.3 2.1 convolution_convert_fusion.3
  98.4 0.0 copy-done.5
  98.4 0.0 copy-start.3
  98.4 3.6 %all-to-all-start.5 = ((bf16[8,32,1024]{2,1,0:T(8,128)(2,1)}), bf16[8,32,1024]{2,1,0:T(8,128)(2,1)S(1)}, u32[]{:S(2)}, u32[]{:S(2)}) async-start(bf16[8,32,1024]{2,1,0:T(8,128)(2,1)} %bitcast.3), calls=%async_computation.5 | async-start | bytes 1048576 | tf_op jit(solution)/shard_map/all_to_all | solution.py:34
  102.0 4.4 %convolution_convert_fusion = bf16[2048,256]{0,1:T(8,128)(2,1)} fusion(bf16[256,1024]{1,0:T(8,128)(2,1)S(1)} %bitcast.29, bf16[1024,2048]{1,0:T(8,128)(2,1)} %copy-done.5), kind=kOutput, calls=%fused_computation.7 | convolution fusion | flops 1074266112 | bytes 5767168 | tf_op jit(solution)/shard_map/dot_general | solution.py:65
  106.4 4.6 %all-to-all-done.5 = bf16[8,32,1024]{2,1,0:T(8,128)(2,1)S(1)} async-done(((bf16[8,32,1024]{2,1,0:T(8,128)(2,1)}), bf16[8,32,1024]{2,1,0:T(8,128)(2,1)S(1)}, u32[]{:S(2)}, u32[]{:S(2)}) %all-to-all-start.5) | async-done | bytes 524320 | tf_op jit(solution)/shard_map/all_to_all | solution.py:34
  111.1 5.8 %all-to-all-start.6 = ((bf16[16,16,2048]{2,1,0:T(8,128)(2,1)}), bf16[16,16,2048]{2,1,0:T(8,128)(2,1)S(1)}, u32[]{:S(2)}, u32[]{:S(2)}) async-start(bf16[16,16,2048]{2,1,0:T(8,128)(2,1)} %bitcast.5), calls=%async_computation.6 | async-start | bytes 2097152 | tf_op jit(solution)/shard_map/all_to_all | solution.py:34
  116.8 0.1 convert_reduce_fusion.5
  116.9 0.0 copy-done.2
  117.0 16.8 %all-to-all-done.6 = bf16[16,16,2048]{2,1,0:T(8,128)(2,1)S(1)} async-done(((bf16[16,16,2048]{2,1,0:T(8,128)(2,1)}), bf16[16,16,2048]{2,1,0:T(8,128)(2,1)S(1)}, u32[]{:S(2)}, u32[]{:S(2)}) %all-to-all-start.6) | async-done | bytes 1048608 | tf_op jit(solution)/shard_map/all_to_all | solution.py:34
  133.8 0.8 broadcast_in_dim.14
  134.6 3.5 %all-to-all-start.8 = ((bf16[8,32,1024]{2,1,0:T(8,128)(2,1)}), bf16[8,32,1024]{2,1,0:T(8,128)(2,1)S(1)}, u32[]{:S(2)}, u32[]{:S(2)}) async-start(bf16[8,32,1024]{2,1,0:T(8,128)(2,1)} %broadcast_in_dim.14), calls=%async_computation.8 | async-start | bytes 1048576 | tf_op jit(solution)/shard_map/all_to_all | solution.py:11
  138.1 0.1 convert_reduce_fusion.3
  138.3 0.0 copy-done.3
  138.3 8.8 %all-to-all-done.8 = bf16[8,32,1024]{2,1,0:T(8,128)(2,1)S(1)} async-done(((bf16[8,32,1024]{2,1,0:T(8,128)(2,1)}), bf16[8,32,1024]{2,1,0:T(8,128)(2,1)S(1)}, u32[]{:S(2)}, u32[]{:S(2)}) %all-to-all-start.8) | async-done | bytes 524320 | tf_op jit(solution)/shard_map/all_to_all | solution.py:11
  147.1 0.1 stack.5
  147.2 22.6 %all_to_all.60 = bf16[16,16,2048]{2,1,0:T(8,128)(2,1)S(1)} all-to-all(bf16[16,16,2048]{2,1,0:T(8,128)(2,1)S(1)} %stack.5), channel_id=1, replica_groups=mesh['row'=16,'col'=8] {'row'}, dimensions={0} | all-to-all | bytes 2097152 | tf_op jit(solution)/shard_map/all_to_all | solution.py:48
  169.9 12.8 %select_convert_fusion = bf16[1024,2048]{1,0:T(8,128)(2,1)S(1)} fusion(s32[1024,2048]{1,0:T(8,128)} %param.5, bf16[256,1024]{1,0:T(8,128)(2,1)S(1)} %bitcast.30, bf16[256,2048]{1,0:T(8,128)(2,1)S(1)} %bitcast.26, f32[2048]{0:T(1024)S(1)} %log.23, f32[1024]{0:T(1024)S(1)} %log.22, f32[]{:T(128)S(6)} %log.21), kind=kOutput, calls=%fused_computation | convolution fusion | flops 1105199104 | bytes 14168068 | tf_op jit(solution)/shard_map/dot_general | solution.py:50
  182.7 0.0 copy-start.4
  182.7 2.1 convolution_convert_fusion.2
  184.8 0.0 copy-done.4
  184.8 3.5 %all-to-all-start.9 = ((bf16[8,32,1024]{2,1,0:T(8,128)(2,1)}), bf16[8,32,1024]{2,1,0:T(8,128)(2,1)S(1)}, u32[]{:S(2)}, u32[]{:S(2)}) async-start(bf16[8,32,1024]{2,1,0:T(8,128)(2,1)} %bitcast.8), calls=%async_computation.9 | async-start | bytes 1048576 | tf_op jit(solution)/shard_map/all_to_all | solution.py:34
  188.3 4.4 %convolution_convert_fusion.1 = bf16[256,2048]{1,0:T(8,128)(2,1)} fusion(bf16[256,1024]{1,0:T(8,128)(2,1)S(1)} %bitcast.31, bf16[1024,2048]{1,0:T(8,128)(2,1)} %copy-done.4), kind=kOutput, calls=%fused_computation.8 | convolution fusion | flops 1074266112 | bytes 5767168 | tf_op jit(solution)/shard_map/dot_general | solution.py:65
  192.8 4.4 %all-to-all-done.9 = bf16[8,32,1024]{2,1,0:T(8,128)(2,1)S(1)} async-done(((bf16[8,32,1024]{2,1,0:T(8,128)(2,1)}), bf16[8,32,1024]{2,1,0:T(8,128)(2,1)S(1)}, u32[]{:S(2)}, u32[]{:S(2)}) %all-to-all-start.9) | async-done | bytes 524320 | tf_op jit(solution)/shard_map/all_to_all | solution.py:34
  197.2 5.5 %all-to-all-start.10 = ((bf16[16,16,2048]{2,1,0:T(8,128)(2,1)}), bf16[16,16,2048]{2,1,0:T(8,128)(2,1)S(1)}, u32[]{:S(2)}, u32[]{:S(2)}) async-start(bf16[16,16,2048]{2,1,0:T(8,128)(2,1)} %bitcast.9), calls=%async_computation.10 | async-start | bytes 2097152 | tf_op jit(solution)/shard_map/all_to_all | solution.py:34
  202.7 0.1 convert_reduce_fusion.4
  202.8 0.7 multiply_subtract_fusion.1
  203.5 16.3 %all-to-all-done.10 = bf16[16,16,2048]{2,1,0:T(8,128)(2,1)S(1)} async-done(((bf16[16,16,2048]{2,1,0:T(8,128)(2,1)}), bf16[16,16,2048]{2,1,0:T(8,128)(2,1)S(1)}, u32[]{:S(2)}, u32[]{:S(2)}) %all-to-all-start.10) | async-done | bytes 1048608 | tf_op jit(solution)/shard_map/all_to_all | solution.py:34
  219.8 0.1 convert_reduce_fusion.2
  220.0 0.7 multiply_subtract_fusion
  (7 shorter events, 0.1 us)
Async XLA Ops:
  0.6 38.1 %copy-start = (f32[32,1024]{1,0:T(8,128)S(1)}, f32[32,1024]{1,0:T(8,128)}, u32[]{:S(2)}) copy-start(f32[32,1024]{1,0:T(8,128)} %param.6) | copy-start | bytes 393220
  0.6 50.1 %copy-start.1 = (f32[16,2048]{1,0:T(8,128)S(1)}, f32[16,2048]{1,0:T(8,128)}, u32[]{:S(2)}) copy-start(f32[16,2048]{1,0:T(8,128)} %param.7) | copy-start | bytes 393220
  34.7 11.7 %all-to-all-start.4 = ((f32[16,1,2048]{2,1,0:T(1,128)}), f32[16,1,2048]{2,1,0:T(1,128)S(1)}, u32[]{:S(2)}, u32[]{:S(2)}) async-start(f32[16,1,2048]{2,1,0:T(1,128)} %broadcast_in_dim.13), calls=%async_computation.4 | async-start | bytes 262144 | tf_op jit(solution)/shard_map/all_to_all | solution.py:11
  47.3 12.9 %all-to-all-start = ((bf16[8,32,1024]{2,1,0:T(8,128)(2,1)}), bf16[8,32,1024]{2,1,0:T(8,128)(2,1)S(1)}, u32[]{:S(2)}, u32[]{:S(2)}) async-start(bf16[8,32,1024]{2,1,0:T(8,128)(2,1)} %broadcast_in_dim.10), calls=%async_computation | async-start | bytes 1048576 | tf_op jit(solution)/shard_map/all_to_all | solution.py:11
  61.2 22.1 %all-to-all-start.1 = ((bf16[16,16,2048]{2,1,0:T(8,128)(2,1)}), bf16[16,16,2048]{2,1,0:T(8,128)(2,1)S(1)}, u32[]{:S(2)}, u32[]{:S(2)}) async-start(bf16[16,16,2048]{2,1,0:T(8,128)(2,1)} %stack.4), calls=%async_computation.1 | async-start | bytes 2097152 | tf_op jit(solution)/shard_map/all_to_all | solution.py:48
  96.2 2.1 copy-start.5
  96.3 20.6 %copy-start.2 = (f32[32,1024]{1,0:T(8,128)S(1)}, f32[32,1024]{1,0:T(8,128)}, u32[]{:S(2)}) copy-start(f32[32,1024]{1,0:T(8,128)} %param.8) | copy-start | bytes 393220
  98.4 39.9 %copy-start.3 = (f32[16,2048]{1,0:T(8,128)S(1)}, f32[16,2048]{1,0:T(8,128)}, u32[]{:S(2)}) copy-start(f32[16,2048]{1,0:T(8,128)} %param.9) | copy-start | bytes 393220
  98.4 12.7 %all-to-all-start.5 = ((bf16[8,32,1024]{2,1,0:T(8,128)(2,1)}), bf16[8,32,1024]{2,1,0:T(8,128)(2,1)S(1)}, u32[]{:S(2)}, u32[]{:S(2)}) async-start(bf16[8,32,1024]{2,1,0:T(8,128)(2,1)} %bitcast.3), calls=%async_computation.5 | async-start | bytes 1048576 | tf_op jit(solution)/shard_map/all_to_all | solution.py:34
  111.1 22.7 %all-to-all-start.6 = ((bf16[16,16,2048]{2,1,0:T(8,128)(2,1)}), bf16[16,16,2048]{2,1,0:T(8,128)(2,1)S(1)}, u32[]{:S(2)}, u32[]{:S(2)}) async-start(bf16[16,16,2048]{2,1,0:T(8,128)(2,1)} %bitcast.5), calls=%async_computation.6 | async-start | bytes 2097152 | tf_op jit(solution)/shard_map/all_to_all | solution.py:34
  134.6 12.5 %all-to-all-start.8 = ((bf16[8,32,1024]{2,1,0:T(8,128)(2,1)}), bf16[8,32,1024]{2,1,0:T(8,128)(2,1)S(1)}, u32[]{:S(2)}, u32[]{:S(2)}) async-start(bf16[8,32,1024]{2,1,0:T(8,128)(2,1)} %broadcast_in_dim.14), calls=%async_computation.8 | async-start | bytes 1048576 | tf_op jit(solution)/shard_map/all_to_all | solution.py:11
  182.7 2.1 copy-start.4
  184.8 12.4 %all-to-all-start.9 = ((bf16[8,32,1024]{2,1,0:T(8,128)(2,1)}), bf16[8,32,1024]{2,1,0:T(8,128)(2,1)S(1)}, u32[]{:S(2)}, u32[]{:S(2)}) async-start(bf16[8,32,1024]{2,1,0:T(8,128)(2,1)} %bitcast.8), calls=%async_computation.9 | async-start | bytes 1048576 | tf_op jit(solution)/shard_map/all_to_all | solution.py:34
  197.2 22.6 %all-to-all-start.10 = ((bf16[16,16,2048]{2,1,0:T(8,128)(2,1)}), bf16[16,16,2048]{2,1,0:T(8,128)(2,1)S(1)}, u32[]{:S(2)}, u32[]{:S(2)}) async-start(bf16[16,16,2048]{2,1,0:T(8,128)(2,1)} %bitcast.9), calls=%async_computation.10 | async-start | bytes 2097152 | tf_op jit(solution)/shard_map/all_to_all | solution.py:34
